TPU v7x, 128 devices: a whole 4x4x4 slice. The times are simulated.
128 devices in a mesh: row: 8 (over x, z_lo), col: 16 (over z_hi, y, core).
Axes of the slice: x: 4, y: 4, z: 4 (z_hi: 2, z_lo: 2; z = z_hi * 2 + z_lo), core: 2. Of those that a mesh axis runs over, the one named last changes fastest.
Arguments:
- factor_tiles: float32 [16, 1024, 8, 2048], P(None, 'row', None, 'col'), may hold values from -40 to 40, as said below
Outputs:
- rotated: float32 [16384, 16384], P(None, ('row', 'col'))
Inputs may be any that keep to these rules, and one draw needn't show every extreme that they name: `factor_tiles`: upper triangular: entries below the diagonal are zero, entries on it are positive.
All inputs are finite; a program needn't handle non-finite values.
Results may differ from a plain program's by a relative error of at most 0.0003.
Values sent between devices are 32-bit elements; how exact they have to be, the bound alone decides.
A program may use at most 128 MiB of HBM per device.

v0:
```python
import jax
import jax.numpy as jnp
from jax import lax
from jax.sharding import PartitionSpec as P

LOGB = 7
OUTER = 4
INNER = 8
damping_ratio = 0.01
highest = lax.Precision.HIGHEST


def passed_along(value, axis, steps):
    count = lax.axis_size(axis)
    leading, last = (max(0, -steps), min(count, count - steps))
    return lax.ppermute(value, axis, [(source, source + steps) for source in range(leading, last)])


def step_rotation(gram_matrix, stride):
    order = gram_matrix.shape[-1]
    index_row = jnp.arange(order)
    partner = jnp.bitwise_xor(index_row, stride)
    is_lead = jnp.bitwise_and(index_row, stride) == 0
    identity = index_row[:, None] == index_row[None, :]
    partner_mask = index_row[None, :] == partner[:, None]
    diagonal = jnp.sum(jnp.where(identity, gram_matrix, 0.0), axis=-1)
    diag_other = jnp.sum(jnp.where(partner_mask, diagonal[..., None, :], 0.0), axis=-1)
    cross_row = jnp.sum(jnp.where(partner_mask, gram_matrix, 0.0), axis=-1)
    cross_col = jnp.sum(jnp.where(partner_mask, gram_matrix, 0.0), axis=-2)
    diag_p = jnp.where(is_lead, diagonal, diag_other)
    diag_q = jnp.where(is_lead, diag_other, diagonal)
    cross = jnp.where(is_lead, cross_row, cross_col)
    diag_gap = diag_q - diag_p
    diag_sum = diag_p + diag_q
    rot_angle = 0.5 * jnp.arctan2(
        2.0 * cross * diag_gap, diag_gap * diag_gap + damping_ratio * diag_sum * diag_sum
    )
    cosine = jnp.cos(rot_angle)
    sine_val = jnp.where(is_lead, -jnp.sin(rot_angle), jnp.sin(rot_angle))
    turn = jnp.where(identity, cosine[..., None, :], 0.0)
    return turn + jnp.where(partner_mask, sine_val[..., None, :], 0.0)


def inner_solve(gram_matrix):
    order = gram_matrix.shape[-1]
    accum = jnp.eye(order, dtype=gram_matrix.dtype)
    for inner_step in range(INNER):
        bit_index = (LOGB - 1 - inner_step) % LOGB
        turn = step_rotation(gram_matrix, 2**bit_index)
        gram_matrix = jnp.einsum("...ik,...kj->...ij", gram_matrix, turn, precision=highest)
        gram_matrix = jnp.einsum("...ki,...kj->...ij", turn, gram_matrix, precision=highest)
        accum = jnp.einsum("...ik,...kj->...ij", accum, turn, precision=highest)
    return accum


def relayout(tile_work):
    cycles, row_count, tile_count, tile_width = tile_work.shape
    split_view = tile_work.reshape(cycles, 1, row_count, tile_count, tile_width)
    received = lax.all_to_all(split_view, "row", split_axis=3, concat_axis=1, tiled=True)
    return received.reshape(cycles * received.shape[1] * row_count, tile_width)


def per_device(factor_tiles):
    half_width = factor_tiles.shape[-1] // 2
    column_block = relayout(factor_tiles)
    position = lax.axis_index(("row", "col"))
    devices_total = lax.axis_size(("row", "col"))
    gram_matrix = jnp.einsum("ni,nj->ij", column_block, column_block, precision=highest)
    rotation = inner_solve(gram_matrix)
    block_lines = jnp.einsum("ni,ij->jn", column_block, rotation, precision=highest)
    for round_index in range(1, OUTER):
        top_half = block_lines[:half_width]
        bottom_half = block_lines[half_width:]
        outgoing = jnp.where(position == 0, bottom_half, top_half)
        arrived = passed_along(outgoing, ("row", "col"), 1)
        behind = passed_along(bottom_half, ("row", "col"), -1)
        new_top = jnp.where(position == 0, top_half, arrived)
        new_bottom = jnp.where(position == devices_total - 1, top_half, behind)
        block_lines = jnp.concatenate([new_top, new_bottom], axis=0)
        gram_matrix = jnp.einsum("in,jn->ij", block_lines, block_lines, precision=highest)
        rotation = inner_solve(gram_matrix)
        if round_index + 1 < OUTER:
            block_lines = jnp.einsum("in,ij->jn", block_lines, rotation, precision=highest)
        else:
            return jnp.einsum("in,ij->nj", block_lines, rotation, precision=highest)


def solution(mesh):
    return jax.shard_map(
        per_device,
        mesh=mesh,
        in_specs=(P(None, "row", None, "col"),),
        out_specs=P(None, ("row", "col")),
        check_vma=False,
    )
```

profile of v0, /device:TPU:25, one launch (start us, length us, event | category | flops | bytes accessed | tf_op | source)
XLA Modules:
  0.0 464.9 jit_solution(8180532006522970439)
XLA Ops:
  0.0 9.3 %copy.7 = f32[16,128,8,128]{1,3,0,2:T(8,128)} copy(f32[16,128,8,128]{3,2,1,0:T(8,128)} %param.1) | data formatting | bytes 16777216 | tf_op args[0]
  9.3 5.4 %all-to-all-start = ((f32[16,1,128,8,128]{2,4,0,1,3:T(8,128)}), f32[16,1,128,8,128]{2,4,0,1,3:T(8,128)}, u32[]{:S(2)}, u32[]{:S(2)}) async-start(f32[16,1,128,8,128]{2,4,0,1,3:T(8,128)} %bitcast.113), calls=%async_computation | async-start | bytes 16777216 | tf_op jit(solution)/shard_map/all_to_all | solution.py:59
  14.7 115.1 %all-to-all-done = f32[16,1,128,8,128]{2,4,0,1,3:T(8,128)} async-done(((f32[16,1,128,8,128]{2,4,0,1,3:T(8,128)}), f32[16,1,128,8,128]{2,4,0,1,3:T(8,128)}, u32[]{:S(2)}, u32[]{:S(2)}) %all-to-all-start) | async-done | bytes 8388640 | tf_op jit(solution)/shard_map/all_to_all | solution.py:59
  129.7 7.9 %copy.30 = f32[16,1,128,8,128]{2,4,3,0,1:T(8,128)} copy(f32[16,1,128,8,128]{2,4,0,1,3:T(8,128)} %all-to-all-done) | data formatting | bytes 16777216 | tf_op jit(solution)/shard_map/all_to_all | solution.py:59
  137.6 9.3 %copy.10 = f32[16,8,1,128,1,128]{5,3,1,0,4,2:T(8,128)} copy(f32[16,8,1,128,1,128]{3,5,1,0,4,2:T(8,128)} %bitcast.114) | data formatting | bytes 16777216 | tf_op jit(solution)/shard_map/all_to_all | solution.py:59
  146.9 10.9 %fusion.152 = (f32[128]{0:T(128)S(1)}, f32[128]{0:T(128)S(1)}, f32[128]{0:T(128)S(1)}, f32[128,128]{0,1:T(8,128)S(1)}) fusion(s32[128]{0:T(128)S(1)} %iota_xor_fusion.6, f32[16,1,128,8,128]{2,4,0,1,3:T(8,128)} %all-to-all-done), kind=kOutput, calls=%fused_computation.257 | convolution fusion | flops 3221339648 | bytes 8456192 | tf_op jit(solution)/shard_map/ni,nj->ij/dot_general | solution.py:68
  159.7 0.4 fusion.176
  160.7 0.4 fusion.184
  161.7 0.4 fusion.192
  162.7 0.4 fusion.200
  167.8 9.3 %fusion.822 = f32[128,16384]{1,0:T(8,128)S(1)} fusion(f32[128,128]{1,0:T(8,128)S(1)} %fusion.90, f32[16384,128]{1,0:T(8,128)S(1)} %bitcast.112), kind=kOutput, calls=%fused_computation.973 | convolution fusion | flops 3221225472 | bytes 16842752 | tf_op jit(solution)/shard_map/ni,ij->jn/dot_general | solution.py:70
  177.1 4.1 slice_select_fusion.8
  181.2 1.8 copy-done
  183.0 6.4 %collective-permute-start = (f32[64,16384]{1,0:T(8,128)}, f32[64,16384]{1,0:T(8,128)}, u32[]{:S(2)}, u32[]{:S(2)}) collective-permute-start(f32[64,16384]{1,0:T(8,128)} %get-tuple-element.175), channel_id=1, source_target_pairs={{0,1},{1,2},{2,3},{3,4},{4,5},{5,6},{6,7},{7,8},{8,9},{9,10},{10,1... | collective-permute-start | bytes 12582920 | tf_op jit(solution)/shard_map/ppermute | solution.py:16
  189.4 1.9 collective-permute-start.1
  191.3 43.8 %collective-permute-done = f32[64,16384]{1,0:T(8,128)} collective-permute-done((f32[64,16384]{1,0:T(8,128)}, f32[64,16384]{1,0:T(8,128)}, u32[]{:S(2)}, u32[]{:S(2)}) %collective-permute-start) | collective-permute-done | bytes 4194336 | tf_op jit(solution)/shard_map/ppermute | solution.py:16
  235.1 8.0 %collective-permute-done.1 = f32[64,16384]{1,0:T(8,128)} collective-permute-done((f32[64,16384]{1,0:T(8,128)}, f32[64,16384]{1,0:T(8,128)}, u32[]{:S(2)}, u32[]{:S(2)}) %collective-permute-start.1) | collective-permute-done | bytes 4194336 | tf_op jit(solution)/shard_map/ppermute | solution.py:16
  243.1 5.3 %slice_select_fusion.7 = (f32[64,16384]{1,0:T(8,128)S(1)}, f32[64,16384]{1,0:T(8,128)S(1)}) fusion(f32[64,16384]{1,0:T(8,128)} %collective-permute-done, f32[128,16384]{1,0:T(8,128)} %copy-done, pred[]{:T(512)S(6)} %eq.1664, f32[64,16384]{1,0:T(8,128)} %collective-permute-done.1, pred[]{:T(512)S(6)} %eq.1694), kind=kLoop, calls=%fused_computation.21 | loop fusion | flops 2097152 | bytes 20971522 | tf_op jit(solution)/shard_map/jit(_where)/select_n | solution.py:77
  248.5 6.7 %fusion.156 = (f32[128]{0:T(128)S(1)}, f32[128]{0:T(128)S(1)}, f32[128]{0:T(128)S(1)}, f32[128,128]{0,1:T(8,128)S(1)}) fusion(s32[128]{0:T(128)S(1)} %iota_xor_fusion.6, f32[64,16384]{1,0:T(8,128)S(1)} %get-tuple-element.174, f32[64,16384]{1,0:T(8,128)S(1)} %get-tuple-element.173), kind=kOutput, calls=%fused_computation.261 | convolution fusion | flops 3223436800 | bytes 8456192 | tf_op jit(solution)/shard_map/in,jn->ij/dot_general | solution.py:80
  256.1 0.4 fusion.170
  257.1 0.4 fusion.178
  259.1 0.4 fusion.194
  262.2 0.6 fusion.158
  265.4 7.7 %fusion.8 = f32[128,16384]{1,0:T(8,128)S(1)} fusion(f32[128,128]{1,0:T(8,128)S(1)} %fusion.65, f32[64,16384]{1,0:T(8,128)S(1)} %copy-done.3, f32[64,16384]{1,0:T(8,128)S(1)} %get-tuple-element.173), kind=kOutput, calls=%fused_computation.12 | convolution fusion | flops 3223322624 | bytes 16842752 | tf_op jit(solution)/shard_map/in,ij->jn/dot_general | solution.py:83
  273.0 0.7 slice_select_fusion.5
  273.8 1.9 collective-permute-start.2
  275.7 2.8 collective-permute-start.3
  278.5 42.6 %collective-permute-done.2 = f32[64,16384]{1,0:T(8,128)S(1)} collective-permute-done((f32[64,16384]{1,0:T(8,128)S(1)}, f32[64,16384]{1,0:T(8,128)S(1)}, u32[]{:S(2)}, u32[]{:S(2)}) %collective-permute-start.2) | collective-permute-done | bytes 4194336 | tf_op jit(solution)/shard_map/ppermute | solution.py:16
  321.1 2.0 copy-done.8
  323.2 6.1 %collective-permute-done.3 = f32[64,16384]{1,0:T(8,128)} collective-permute-done((f32[64,16384]{1,0:T(8,128)S(1)}, f32[64,16384]{1,0:T(8,128)}, u32[]{:S(2)}, u32[]{:S(2)}) %collective-permute-start.3) | collective-permute-done | bytes 4194336 | tf_op jit(solution)/shard_map/ppermute | solution.py:16
  329.3 6.2 %slice_select_fusion.4 = (f32[64,16384]{1,0:T(8,128)S(1)}, f32[64,16384]{1,0:T(8,128)}) fusion(f32[64,16384]{1,0:T(8,128)} %copy-done.8, f32[128,16384]{1,0:T(8,128)S(1)} %fusion.8, pred[]{:T(512)S(6)} %eq.1664, f32[64,16384]{1,0:T(8,128)} %collective-permute-done.3, pred[]{:T(512)S(6)} %eq.1694), kind=kLoop, calls=%fused_computation.18 | loop fusion | flops 2097152 | bytes 20971522 | tf_op jit(solution)/shard_map/jit(_where)/select_n | solution.py:77
  335.4 11.7 %fusion.160 = (f32[128]{0:T(128)S(1)}, f32[128]{0:T(128)S(1)}, f32[128]{0:T(128)S(1)}, f32[128,128]{0,1:T(8,128)S(1)}) fusion(s32[128]{0:T(128)S(1)} %iota_xor_fusion.6, f32[64,16384]{1,0:T(8,128)} %get-tuple-element.170, f32[64,16384]{1,0:T(8,128)S(1)} %get-tuple-element.169), kind=kOutput, calls=%fused_computation.265 | convolution fusion | flops 3223436800 | bytes 8456192 | tf_op jit(solution)/shard_map/in,jn->ij/dot_general | solution.py:80
  348.0 0.4 fusion.172
  349.0 0.4 fusion.180
  351.0 0.4 fusion.196
  354.1 0.6 fusion.162
  357.3 9.2 %fusion.6 = f32[128,16384]{1,0:T(8,128)S(1)} fusion(f32[128,128]{1,0:T(8,128)S(1)} %fusion.40, f32[64,16384]{1,0:T(8,128)} %get-tuple-element.170, f32[64,16384]{1,0:T(8,128)S(1)} %copy-done.5), kind=kOutput, calls=%fused_computation.10 | convolution fusion | flops 3223322624 | bytes 16842752 | tf_op jit(solution)/shard_map/in,ij->jn/dot_general | solution.py:83
  366.5 0.7 slice_select_fusion.2
  367.2 1.9 collective-permute-start.4
  369.2 2.4 collective-permute-start.5
  371.6 43.0 %collective-permute-done.4 = f32[64,16384]{1,0:T(8,128)S(1)} collective-permute-done((f32[64,16384]{1,0:T(8,128)S(1)}, f32[64,16384]{1,0:T(8,128)S(1)}, u32[]{:S(2)}, u32[]{:S(2)}) %collective-permute-start.4) | collective-permute-done | bytes 4194336 | tf_op jit(solution)/shard_map/ppermute | solution.py:16
  414.6 2.0 copy-done.7
  416.6 6.1 %collective-permute-done.5 = f32[64,16384]{1,0:T(8,128)} collective-permute-done((f32[64,16384]{1,0:T(8,128)S(1)}, f32[64,16384]{1,0:T(8,128)}, u32[]{:S(2)}, u32[]{:S(2)}) %collective-permute-start.5) | collective-permute-done | bytes 4194336 | tf_op jit(solution)/shard_map/ppermute | solution.py:16
  422.7 6.2 %slice_select_fusion.1 = (f32[64,16384]{1,0:T(8,128)S(1)}, f32[64,16384]{1,0:T(8,128)}) fusion(f32[64,16384]{1,0:T(8,128)} %copy-done.7, f32[128,16384]{1,0:T(8,128)S(1)} %fusion.6, pred[]{:T(512)S(6)} %eq.1664, f32[64,16384]{1,0:T(8,128)} %collective-permute-done.5, pred[]{:T(512)S(6)} %eq.1694), kind=kLoop, calls=%fused_computation.15 | loop fusion | flops 2097152 | bytes 20971522 | tf_op jit(solution)/shard_map/jit(_where)/select_n | solution.py:77
  428.9 10.2 %fusion.164 = (f32[128]{0:T(128)S(1)}, f32[128]{0:T(128)S(1)}, f32[128]{0:T(128)S(1)}, f32[128,128]{0,1:T(8,128)S(1)}) fusion(s32[128]{0:T(128)S(1)} %iota_xor_fusion.6, f32[64,16384]{1,0:T(8,128)} %get-tuple-element.166, f32[64,16384]{1,0:T(8,128)S(1)} %get-tuple-element.165), kind=kOutput, calls=%fused_computation.269 | convolution fusion | flops 3223436800 | bytes 8456192 | tf_op jit(solution)/shard_map/in,jn->ij/dot_general | solution.py:80
  443.0 0.4 fusion.198
  446.0 0.6 fusion.166
  449.3 15.4 %fusion.4 = f32[16384,128]{1,0:T(8,128)} fusion(f32[128,128]{1,0:T(8,128)S(1)} %fusion.15, f32[64,16384]{1,0:T(8,128)S(1)} %copy-done.1, f32[64,16384]{1,0:T(8,128)S(1)} %get-tuple-element.165), kind=kOutput, calls=%fused_computation.8 | convolution fusion | flops 3223322624 | bytes 16842752 | tf_op jit(solution)/shard_map/in,ij->nj/dot_general | solution.py:85
  (189 shorter events, 33.4 us)
Async XLA Ops:
  9.3 120.5 %all-to-all-start = ((f32[16,1,128,8,128]{2,4,0,1,3:T(8,128)}), f32[16,1,128,8,128]{2,4,0,1,3:T(8,128)}, u32[]{:S(2)}, u32[]{:S(2)}) async-start(f32[16,1,128,8,128]{2,4,0,1,3:T(8,128)} %bitcast.113), calls=%async_computation | async-start | bytes 16777216 | tf_op jit(solution)/shard_map/all_to_all | solution.py:59
  146.9 20.9 %copy-start.6 = (f32[16,8,1,128,1,128]{5,3,1,0,4,2:T(8,128)S(1)}, f32[16,8,1,128,1,128]{5,3,1,0,4,2:T(8,128)}, u32[]{:S(2)}) copy-start(f32[16,8,1,128,1,128]{5,3,1,0,4,2:T(8,128)} %copy.10) | copy-start | bytes 25165828
  177.1 5.9 %copy-start = (f32[128,16384]{1,0:T(8,128)}, f32[128,16384]{1,0:T(8,128)S(1)}, u32[]{:S(2)}) copy-start(f32[128,16384]{1,0:T(8,128)S(1)} %fusion.822) | copy-start | bytes 25165828
  183.0 52.1 %collective-permute-start = (f32[64,16384]{1,0:T(8,128)}, f32[64,16384]{1,0:T(8,128)}, u32[]{:S(2)}, u32[]{:S(2)}) collective-permute-start(f32[64,16384]{1,0:T(8,128)} %get-tuple-element.175), channel_id=1, source_target_pairs={{0,1},{1,2},{2,3},{3,4},{4,5},{5,6},{6,7},{7,8},{8,9},{9,10},{10,1... | collective-permute-start | bytes 12582920 | tf_op jit(solution)/shard_map/ppermute | solution.py:16
  189.4 53.8 %collective-permute-start.1 = (f32[64,16384]{1,0:T(8,128)}, f32[64,16384]{1,0:T(8,128)}, u32[]{:S(2)}, u32[]{:S(2)}) collective-permute-start(f32[64,16384]{1,0:T(8,128)} %get-tuple-element.176), channel_id=1, source_target_pairs={{1,0},{2,1},{3,2},{4,3},{5,4},{6,5},{7,6},{8,7},{9,8},{10,9},{11,1... | collective-permute-start | bytes 12582920 | tf_op jit(solution)/shard_map/ppermute | solution.py:16
  248.5 6.7 %copy-start.2 = (f32[64,16384]{1,0:T(8,128)}, f32[64,16384]{1,0:T(8,128)S(1)}, u32[]{:S(2)}) copy-start(f32[64,16384]{1,0:T(8,128)S(1)} %get-tuple-element.174) | copy-start | bytes 12582916
  255.2 10.2 %copy-start.3 = (f32[64,16384]{1,0:T(8,128)S(1)}, f32[64,16384]{1,0:T(8,128)}, u32[]{:S(2)}) copy-start(f32[64,16384]{1,0:T(8,128)} %copy-done.2) | copy-start | bytes 12582916
  273.8 47.4 %collective-permute-start.2 = (f32[64,16384]{1,0:T(8,128)S(1)}, f32[64,16384]{1,0:T(8,128)S(1)}, u32[]{:S(2)}, u32[]{:S(2)}) collective-permute-start(f32[64,16384]{1,0:T(8,128)S(1)} %get-tuple-element.171), channel_id=1, source_target_pairs={{0,1},{1,2},{2,3},{3,4},{4,5},{5,6},{6,7},{7,8},{8,9},{9,10},{10,1... | collective-permute-start | bytes 12582920 | tf_op jit(solution)/shard_map/ppermute | solution.py:16
  275.7 53.5 %collective-permute-start.3 = (f32[64,16384]{1,0:T(8,128)S(1)}, f32[64,16384]{1,0:T(8,128)}, u32[]{:S(2)}, u32[]{:S(2)}) collective-permute-start(f32[64,16384]{1,0:T(8,128)S(1)} %get-tuple-element.172), channel_id=1, source_target_pairs={{1,0},{2,1},{3,2},{4,3},{5,4},{6,5},{7,6},{8,7},{9,8},{10,9},{11,1... | collective-permute-start | bytes 12582920 | tf_op jit(solution)/shard_map/ppermute | solution.py:16
  321.1 2.0 copy-start.8
  335.4 11.7 %copy-start.4 = (f32[64,16384]{1,0:T(8,128)}, f32[64,16384]{1,0:T(8,128)S(1)}, u32[]{:S(2)}) copy-start(f32[64,16384]{1,0:T(8,128)S(1)} %get-tuple-element.169) | copy-start | bytes 12582916
  347.1 10.2 %copy-start.5 = (f32[64,16384]{1,0:T(8,128)S(1)}, f32[64,16384]{1,0:T(8,128)}, u32[]{:S(2)}) copy-start(f32[64,16384]{1,0:T(8,128)} %copy-done.4) | copy-start | bytes 12582916
  367.2 47.4 %collective-permute-start.4 = (f32[64,16384]{1,0:T(8,128)S(1)}, f32[64,16384]{1,0:T(8,128)S(1)}, u32[]{:S(2)}, u32[]{:S(2)}) collective-permute-start(f32[64,16384]{1,0:T(8,128)S(1)} %get-tuple-element.167), channel_id=1, source_target_pairs={{0,1},{1,2},{2,3},{3,4},{4,5},{5,6},{6,7},{7,8},{8,9},{9,10},{10,1... | collective-permute-start | bytes 12582920 | tf_op jit(solution)/shard_map/ppermute | solution.py:16
  369.2 53.5 %collective-permute-start.5 = (f32[64,16384]{1,0:T(8,128)S(1)}, f32[64,16384]{1,0:T(8,128)}, u32[]{:S(2)}, u32[]{:S(2)}) collective-permute-start(f32[64,16384]{1,0:T(8,128)S(1)} %get-tuple-element.168), channel_id=1, source_target_pairs={{1,0},{2,1},{3,2},{4,3},{5,4},{6,5},{7,6},{8,7},{9,8},{10,9},{11,1... | collective-permute-start | bytes 12582920 | tf_op jit(solution)/shard_map/ppermute | solution.py:16
  414.6 2.0 copy-start.7
  439.1 10.2 %copy-start.1 = (f32[64,16384]{1,0:T(8,128)S(1)}, f32[64,16384]{1,0:T(8,128)}, u32[]{:S(2)}) copy-start(f32[64,16384]{1,0:T(8,128)} %get-tuple-element.166) | copy-start | bytes 12582916
where the time goes:
time: 470 us; the launch traced here: 465 us
  waiting for transfers between devices  265 us (56%)
  matrix products  114 us (24%)
  local copies, waits for them, and re-layouts  32.3 us (7%)
  other arithmetic  30.5 us (6%)
  starting transfers between devices  22.7 us (5%)
    ppermute x6, waiting for transfers between devices, passed_along(): lax.ppermute(value, axis, [(source, source + steps) for source in range(l...  150 us
    all_to_all x1, waiting for transfers between devices, relayout(): lax.all_to_all(split_view, 'row', split_axis=3, concat_axis=1, tiled=True)  115 us
    dot_general x3, matrix products, per_device(): jnp.einsum('in,jn->ij', block_lines, block_lines, precision=highest)  28.6 us
    select_n x3, other arithmetic, per_device(): new_top = jnp.where(position == 0, top_half, arrived)  17.7 us
    ppermute x6, starting transfers between devices, passed_along(): lax.ppermute(value, axis, [(source, source + steps) for source in range(l...  17.4 us
    all_to_all x2, local copies, waits for them, and re-layouts, relayout(): lax.all_to_all(split_view, 'row', split_axis=3, concat_axis=1, tiled=True)  17.2 us
    dot_general x2, matrix products, per_device(): jnp.einsum('in,ij->jn', block_lines, rotation, precision=highest)  16.9 us
    dot_general x1, matrix products, per_device(): return jnp.einsum('in,ij->nj', block_lines, rotation, precision=highest)  15.4 us
  transfers between devices with their start and end apart: 7, of which 7 were waited for; matrix products, arithmetic and copies ran while one was open for 0% of the time, Pallas kernels for 0%

commit v1 on v0

--- a/solution.py
+++ b/solution.py
@@ -56,7 +56,10 @@
 def relayout(tile_work):
     cycles, row_count, tile_count, tile_width = tile_work.shape
     split_view = tile_work.reshape(cycles, 1, row_count, tile_count, tile_width)
-    received = lax.all_to_all(split_view, "row", split_axis=3, concat_axis=1, tiled=True)
+    received = jnp.concatenate(
+        lax.all_to_all(jnp.stack(jnp.split(split_view, lax.axis_size("row"), axis=3)), "row", 0, 0),
+        axis=1,
+    )
     return received.reshape(cycles * received.shape[1] * row_count, tile_width)
 
 

time: 470 us -> 485 us (1.032)
  local copies, waits for them, and re-layouts: 32.3 us -> 46.6 us
    unnamed x19 -> x22, local copies, waits for them, and re-layouts: 15.1 us -> 28.4 us
    all_to_all x2 -> x1, local copies, waits for them, and re-layouts: 17.2 us -> 7.89 us  [relayout(): lax.all_to_all(jnp.stack(jnp.split(split_view, lax.axis_size('row'), axis...]
    reshape x0 -> x1, local copies, waits for them, and re-layouts: none -> 9.26 us  [relayout(): jnp.concatenate(lax.all_to_all(jnp.stack(jnp.split(split_view, lax.axis_s...]
where the time goes in v1:
time: 485 us; the launch traced here: 480 us
  waiting for transfers between devices  265 us (55%)
  matrix products  114 us (24%)
  local copies, waits for them, and re-layouts  46.6 us (10%)
  other arithmetic  30.6 us (6%)
  starting transfers between devices  22.5 us (5%)
    ppermute x6, waiting for transfers between devices, passed_along(): lax.ppermute(value, axis, [(source, source + steps) for source in range(l...  150 us
    all_to_all x1, waiting for transfers between devices, relayout(): lax.all_to_all(jnp.stack(jnp.split(split_view, lax.axis_size('row'), axis...  115 us
    unnamed x22, local copies, waits for them, and re-layouts  28.4 us
    dot_general x3, matrix products, per_device(): jnp.einsum('in,jn->ij', block_lines, block_lines, precision=highest)  27.3 us
    dot_general x2, matrix products, per_device(): jnp.einsum('in,ij->jn', block_lines, rotation, precision=highest)  18.3 us
    select_n x3, other arithmetic, per_device(): new_top = jnp.where(position == 0, top_half, arrived)  17.7 us
    ppermute x6, starting transfers between devices, passed_along(): lax.ppermute(value, axis, [(source, source + steps) for source in range(l...  17.1 us
    dot_general x1, matrix products, per_device(): return jnp.einsum('in,ij->nj', block_lines, rotation, precision=highest)  15.4 us
  transfers between devices with their start and end apart: 7, of which 7 were waited for; matrix products, arithmetic and copies ran while one was open for 0% of the time, Pallas kernels for 0%

profile of v1, /device:TPU:25, one launch (start us, length us, event | category | flops | bytes accessed | tf_op | source)
XLA Modules:
  0.0 479.6 jit_solution(9435263857929486354)
XLA Ops:
  0.0 9.3 %copy.21 = f32[16,128,8,128]{1,3,0,2:T(8,128)} copy(f32[16,128,8,128]{3,2,1,0:T(8,128)} %param.1) | data formatting | bytes 16777216 | tf_op args[0]
  9.3 2.5 fusion.22
  11.8 2.8 fusion.21
  14.6 2.3 fusion.20
  16.9 2.3 fusion.19
  19.2 1.1 fusion.18
  20.4 1.1 fusion.17
  21.5 1.1 fusion.16
  22.5 1.1 fusion.15
  23.6 5.4 %all-to-all-start = ((f32[8,16,1,128,1,128]{3,5,1,4,2,0:T(8,128)}), f32[8,16,1,128,1,128]{3,5,1,4,2,0:T(8,128)}, u32[]{:S(2)}, u32[]{:S(2)}) async-start(f32[8,16,1,128,1,128]{3,5,1,4,2,0:T(8,128)} %fusion.15), calls=%async_computation | async-start | bytes 16777216 | tf_op jit(solution)/shard_map/all_to_all | solution.py:60
  29.0 115.1 %all-to-all-done = f32[8,16,1,128,1,128]{3,5,1,4,2,0:T(8,128)} async-done(((f32[8,16,1,128,1,128]{3,5,1,4,2,0:T(8,128)}), f32[8,16,1,128,1,128]{3,5,1,4,2,0:T(8,128)}, u32[]{:S(2)}, u32[]{:S(2)}) %all-to-all-start) | async-done | bytes 8388640 | tf_op jit(solution)/shard_map/all_to_all | solution.py:60
  144.1 7.9 %copy.44 = f32[8,16,1,128,1,128]{3,5,0,1,4,2:T(8,128)} copy(f32[8,16,1,128,1,128]{3,5,1,4,2,0:T(8,128)} %all-to-all-done) | data formatting | bytes 16777216 | tf_op jit(solution)/shard_map/all_to_all | solution.py:60
  152.0 9.3 %copy.24 = f32[16,8,1,128,1,128]{5,3,1,0,4,2:T(8,128)} copy(f32[16,8,1,128,1,128]{3,5,1,0,4,2:T(8,128)} %bitcast.151) | data formatting | bytes 16777216 | tf_op jit(solution)/shard_map/reshape | solution.py:59
  161.3 10.9 %fusion.160 = (f32[128]{0:T(128)S(1)}, f32[128]{0:T(128)S(1)}, f32[128]{0:T(128)S(1)}, f32[128,128]{0,1:T(8,128)S(1)}) fusion(s32[128]{0:T(128)S(1)} %iota_xor_fusion.6, f32[8,16,1,128,1,128]{3,5,1,4,2,0:T(8,128)} %all-to-all-done), kind=kOutput, calls=%fused_computation.273 | convolution fusion | flops 3221339648 | bytes 8456192 | tf_op jit(solution)/shard_map/ni,nj->ij/dot_general | solution.py:71
  182.1 9.3 %fusion.830 = f32[128,16384]{1,0:T(8,128)S(1)} fusion(f32[128,128]{1,0:T(8,128)S(1)} %fusion.98, f32[16384,128]{1,0:T(8,128)S(1)} %bitcast.150), kind=kOutput, calls=%fused_computation.989 | convolution fusion | flops 3221225472 | bytes 16842752 | tf_op jit(solution)/shard_map/ni,ij->jn/dot_general | solution.py:73
  191.5 4.1 slice_select_fusion.8
  195.6 1.8 copy-done
  197.4 6.4 %collective-permute-start = (f32[64,16384]{1,0:T(8,128)}, f32[64,16384]{1,0:T(8,128)}, u32[]{:S(2)}, u32[]{:S(2)}) collective-permute-start(f32[64,16384]{1,0:T(8,128)} %get-tuple-element.175), channel_id=1, source_target_pairs={{0,1},{1,2},{2,3},{3,4},{4,5},{5,6},{6,7},{7,8},{8,9},{9,10},{10,1... | collective-permute-start | bytes 12582920 | tf_op jit(solution)/shard_map/ppermute | solution.py:16
  203.7 1.9 collective-permute-start.1
  205.7 43.8 %collective-permute-done = f32[64,16384]{1,0:T(8,128)} collective-permute-done((f32[64,16384]{1,0:T(8,128)}, f32[64,16384]{1,0:T(8,128)}, u32[]{:S(2)}, u32[]{:S(2)}) %collective-permute-start) | collective-permute-done | bytes 4194336 | tf_op jit(solution)/shard_map/ppermute | solution.py:16
  249.5 8.0 %collective-permute-done.1 = f32[64,16384]{1,0:T(8,128)} collective-permute-done((f32[64,16384]{1,0:T(8,128)}, f32[64,16384]{1,0:T(8,128)}, u32[]{:S(2)}, u32[]{:S(2)}) %collective-permute-start.1) | collective-permute-done | bytes 4194336 | tf_op jit(solution)/shard_map/ppermute | solution.py:16
  257.5 5.3 %slice_select_fusion.7 = (f32[64,16384]{1,0:T(8,128)S(1)}, f32[64,16384]{1,0:T(8,128)S(1)}) fusion(f32[64,16384]{1,0:T(8,128)} %collective-permute-done, f32[128,16384]{1,0:T(8,128)} %copy-done, pred[]{:T(512)S(6)} %eq.1664, f32[64,16384]{1,0:T(8,128)} %collective-permute-done.1, pred[]{:T(512)S(6)} %eq.1694), kind=kLoop, calls=%fused_computation.21 | loop fusion | flops 2097152 | bytes 20971522 | tf_op jit(solution)/shard_map/jit(_where)/select_n | solution.py:80
  262.8 6.7 %fusion.164 = (f32[128]{0:T(128)S(1)}, f32[128]{0:T(128)S(1)}, f32[128]{0:T(128)S(1)}, f32[128,128]{0,1:T(8,128)S(1)}) fusion(s32[128]{0:T(128)S(1)} %iota_xor_fusion.6, f32[64,16384]{1,0:T(8,128)S(1)} %get-tuple-element.174, f32[64,16384]{1,0:T(8,128)S(1)} %get-tuple-element.173), kind=kOutput, calls=%fused_computation.277 | convolution fusion | flops 3223436800 | bytes 8456192 | tf_op jit(solution)/shard_map/in,jn->ij/dot_general | solution.py:83
  273.5 0.4 fusion.202
  276.5 0.6 fusion.166
  279.7 9.2 %fusion.8 = f32[128,16384]{1,0:T(8,128)S(1)} fusion(f32[128,128]{1,0:T(8,128)S(1)} %fusion.73, f32[64,16384]{1,0:T(8,128)} %copy-done.2, f32[64,16384]{1,0:T(8,128)S(1)} %get-tuple-element.173), kind=kOutput, calls=%fused_computation.12 | convolution fusion | flops 3223322624 | bytes 16842752 | tf_op jit(solution)/shard_map/in,ij->jn/dot_general | solution.py:86
  288.9 0.7 slice_select_fusion.5
  289.6 1.9 collective-permute-start.2
  291.6 2.4 collective-permute-start.3
  294.0 43.0 %collective-permute-done.2 = f32[64,16384]{1,0:T(8,128)S(1)} collective-permute-done((f32[64,16384]{1,0:T(8,128)S(1)}, f32[64,16384]{1,0:T(8,128)S(1)}, u32[]{:S(2)}, u32[]{:S(2)}) %collective-permute-start.2) | collective-permute-done | bytes 4194336 | tf_op jit(solution)/shard_map/ppermute | solution.py:16
  337.0 2.0 copy-done.6
  339.0 6.1 %collective-permute-done.3 = f32[64,16384]{1,0:T(8,128)} collective-permute-done((f32[64,16384]{1,0:T(8,128)S(1)}, f32[64,16384]{1,0:T(8,128)}, u32[]{:S(2)}, u32[]{:S(2)}) %collective-permute-start.3) | collective-permute-done | bytes 4194336 | tf_op jit(solution)/shard_map/ppermute | solution.py:16
  345.1 6.2 %slice_select_fusion.4 = (f32[64,16384]{1,0:T(8,128)S(1)}, f32[64,16384]{1,0:T(8,128)}) fusion(f32[64,16384]{1,0:T(8,128)} %copy-done.6, f32[128,16384]{1,0:T(8,128)S(1)} %fusion.8, pred[]{:T(512)S(6)} %eq.1664, f32[64,16384]{1,0:T(8,128)} %collective-permute-done.3, pred[]{:T(512)S(6)} %eq.1694), kind=kLoop, calls=%fused_computation.18 | loop fusion | flops 2097152 | bytes 20971522 | tf_op jit(solution)/shard_map/jit(_where)/select_n | solution.py:80
  351.3 10.2 %fusion.168 = (f32[128]{0:T(128)S(1)}, f32[128]{0:T(128)S(1)}, f32[128]{0:T(128)S(1)}, f32[128,128]{0,1:T(8,128)S(1)}) fusion(s32[128]{0:T(128)S(1)} %iota_xor_fusion.6, f32[64,16384]{1,0:T(8,128)} %get-tuple-element.170, f32[64,16384]{1,0:T(8,128)S(1)} %get-tuple-element.169), kind=kOutput, calls=%fused_computation.281 | convolution fusion | flops 3223436800 | bytes 8456192 | tf_op jit(solution)/shard_map/in,jn->ij/dot_general | solution.py:83
  365.4 0.4 fusion.204
  368.4 0.8 fusion.170
  371.9 9.2 %fusion.6 = f32[128,16384]{1,0:T(8,128)S(1)} fusion(f32[128,128]{1,0:T(8,128)S(1)} %fusion.48, f32[64,16384]{1,0:T(8,128)} %get-tuple-element.170, f32[64,16384]{1,0:T(8,128)S(1)} %get-tuple-element.169), kind=kOutput, calls=%fused_computation.10 | convolution fusion | flops 3223322624 | bytes 16842752 | tf_op jit(solution)/shard_map/in,ij->jn/dot_general | solution.py:86
  381.0 0.7 slice_select_fusion.2
  381.8 1.9 collective-permute-start.4
  383.7 2.6 collective-permute-start.5
  386.3 42.8 %collective-permute-done.4 = f32[64,16384]{1,0:T(8,128)S(1)} collective-permute-done((f32[64,16384]{1,0:T(8,128)S(1)}, f32[64,16384]{1,0:T(8,128)S(1)}, u32[]{:S(2)}, u32[]{:S(2)}) %collective-permute-start.4) | collective-permute-done | bytes 4194336 | tf_op jit(solution)/shard_map/ppermute | solution.py:16
  429.1 2.0 copy-done.5
  431.2 6.1 %collective-permute-done.5 = f32[64,16384]{1,0:T(8,128)} collective-permute-done((f32[64,16384]{1,0:T(8,128)S(1)}, f32[64,16384]{1,0:T(8,128)}, u32[]{:S(2)}, u32[]{:S(2)}) %collective-permute-start.5) | collective-permute-done | bytes 4194336 | tf_op jit(solution)/shard_map/ppermute | solution.py:16
  437.3 6.2 %slice_select_fusion.1 = (f32[64,16384]{1,0:T(8,128)S(1)}, f32[64,16384]{1,0:T(8,128)}) fusion(f32[64,16384]{1,0:T(8,128)} %copy-done.5, f32[128,16384]{1,0:T(8,128)S(1)} %fusion.6, pred[]{:T(512)S(6)} %eq.1664, f32[64,16384]{1,0:T(8,128)} %collective-permute-done.5, pred[]{:T(512)S(6)} %eq.1694), kind=kLoop, calls=%fused_computation.15 | loop fusion | flops 2097152 | bytes 20971522 | tf_op jit(solution)/shard_map/jit(_where)/select_n | solution.py:80
  443.4 10.3 %fusion.172 = (f32[128]{0:T(128)S(1)}, f32[128]{0:T(128)S(1)}, f32[128]{0:T(128)S(1)}, f32[128,128]{0,1:T(8,128)S(1)}) fusion(s32[128]{0:T(128)S(1)} %iota_xor_fusion.6, f32[64,16384]{1,0:T(8,128)} %get-tuple-element.166, f32[64,16384]{1,0:T(8,128)S(1)} %get-tuple-element.165), kind=kOutput, calls=%fused_computation.285 | convolution fusion | flops 3223436800 | bytes 8456192 | tf_op jit(solution)/shard_map/in,jn->ij/dot_general | solution.py:83
  457.7 0.4 fusion.206
  460.7 0.6 fusion.174
  464.0 15.4 %fusion.4 = f32[16384,128]{1,0:T(8,128)} fusion(f32[128,128]{1,0:T(8,128)S(1)} %fusion.23, f32[64,16384]{1,0:T(8,128)S(1)} %copy-done.1, f32[64,16384]{1,0:T(8,128)S(1)} %get-tuple-element.165), kind=kOutput, calls=%fused_computation.8 | convolution fusion | flops 3223322624 | bytes 16842752 | tf_op jit(solution)/shard_map/in,ij->nj/dot_general | solution.py:88
  (193 shorter events, 36.8 us)
Async XLA Ops:
  9.3 10.0 %copy-start.3 = (f32[16,128,8,128]{1,3,0,2:T(8,128)S(1)}, f32[16,128,8,128]{1,3,0,2:T(8,128)}, u32[]{:S(2)}) copy-start(f32[16,128,8,128]{1,3,0,2:T(8,128)} %copy.21) | copy-start | bytes 25165828
  23.6 120.5 %all-to-all-start = ((f32[8,16,1,128,1,128]{3,5,1,4,2,0:T(8,128)}), f32[8,16,1,128,1,128]{3,5,1,4,2,0:T(8,128)}, u32[]{:S(2)}, u32[]{:S(2)}) async-start(f32[8,16,1,128,1,128]{3,5,1,4,2,0:T(8,128)} %fusion.15), calls=%async_computation | async-start | bytes 16777216 | tf_op jit(solution)/shard_map/all_to_all | solution.py:60
  161.3 20.9 %copy-start.4 = (f32[16,8,1,128,1,128]{5,3,1,0,4,2:T(8,128)S(1)}, f32[16,8,1,128,1,128]{5,3,1,0,4,2:T(8,128)}, u32[]{:S(2)}) copy-start(f32[16,8,1,128,1,128]{5,3,1,0,4,2:T(8,128)} %copy.24) | copy-start | bytes 25165828
  191.4 5.9 %copy-start = (f32[128,16384]{1,0:T(8,128)}, f32[128,16384]{1,0:T(8,128)S(1)}, u32[]{:S(2)}) copy-start(f32[128,16384]{1,0:T(8,128)S(1)} %fusion.830) | copy-start | bytes 25165828
  197.4 52.1 %collective-permute-start = (f32[64,16384]{1,0:T(8,128)}, f32[64,16384]{1,0:T(8,128)}, u32[]{:S(2)}, u32[]{:S(2)}) collective-permute-start(f32[64,16384]{1,0:T(8,128)} %get-tuple-element.175), channel_id=1, source_target_pairs={{0,1},{1,2},{2,3},{3,4},{4,5},{5,6},{6,7},{7,8},{8,9},{9,10},{10,1... | collective-permute-start | bytes 12582920 | tf_op jit(solution)/shard_map/ppermute | solution.py:16
  203.7 53.8 %collective-permute-start.1 = (f32[64,16384]{1,0:T(8,128)}, f32[64,16384]{1,0:T(8,128)}, u32[]{:S(2)}, u32[]{:S(2)}) collective-permute-start(f32[64,16384]{1,0:T(8,128)} %get-tuple-element.176), channel_id=1, source_target_pairs={{1,0},{2,1},{3,2},{4,3},{5,4},{6,5},{7,6},{8,7},{9,8},{10,9},{11,1... | collective-permute-start | bytes 12582920 | tf_op jit(solution)/shard_map/ppermute | solution.py:16
  262.8 16.6 %copy-start.2 = (f32[64,16384]{1,0:T(8,128)}, f32[64,16384]{1,0:T(8,128)S(1)}, u32[]{:S(2)}) copy-start(f32[64,16384]{1,0:T(8,128)S(1)} %get-tuple-element.174) | copy-start | bytes 12582916
  289.6 47.4 %collective-permute-start.2 = (f32[64,16384]{1,0:T(8,128)S(1)}, f32[64,16384]{1,0:T(8,128)S(1)}, u32[]{:S(2)}, u32[]{:S(2)}) collective-permute-start(f32[64,16384]{1,0:T(8,128)S(1)} %get-tuple-element.171), channel_id=1, source_target_pairs={{0,1},{1,2},{2,3},{3,4},{4,5},{5,6},{6,7},{7,8},{8,9},{9,10},{10,1... | collective-permute-start | bytes 12582920 | tf_op jit(solution)/shard_map/ppermute | solution.py:16
  291.6 53.5 %collective-permute-start.3 = (f32[64,16384]{1,0:T(8,128)S(1)}, f32[64,16384]{1,0:T(8,128)}, u32[]{:S(2)}, u32[]{:S(2)}) collective-permute-start(f32[64,16384]{1,0:T(8,128)S(1)} %get-tuple-element.172), channel_id=1, source_target_pairs={{1,0},{2,1},{3,2},{4,3},{5,4},{6,5},{7,6},{8,7},{9,8},{10,9},{11,1... | collective-permute-start | bytes 12582920 | tf_op jit(solution)/shard_map/ppermute | solution.py:16
  337.0 2.0 copy-start.6
  381.8 47.4 %collective-permute-start.4 = (f32[64,16384]{1,0:T(8,128)S(1)}, f32[64,16384]{1,0:T(8,128)S(1)}, u32[]{:S(2)}, u32[]{:S(2)}) collective-permute-start(f32[64,16384]{1,0:T(8,128)S(1)} %get-tuple-element.167), channel_id=1, source_target_pairs={{0,1},{1,2},{2,3},{3,4},{4,5},{5,6},{6,7},{7,8},{8,9},{9,10},{10,1... | collective-permute-start | bytes 12582920 | tf_op jit(solution)/shard_map/ppermute | solution.py:16
  383.7 53.5 %collective-permute-start.5 = (f32[64,16384]{1,0:T(8,128)S(1)}, f32[64,16384]{1,0:T(8,128)}, u32[]{:S(2)}, u32[]{:S(2)}) collective-permute-start(f32[64,16384]{1,0:T(8,128)S(1)} %get-tuple-element.168), channel_id=1, source_target_pairs={{1,0},{2,1},{3,2},{4,3},{5,4},{6,5},{7,6},{8,7},{9,8},{10,9},{11,1... | collective-permute-start | bytes 12582920 | tf_op jit(solution)/shard_map/ppermute | solution.py:16
  429.1 2.0 copy-start.5
  443.4 20.5 %copy-start.1 = (f32[64,16384]{1,0:T(8,128)S(1)}, f32[64,16384]{1,0:T(8,128)}, u32[]{:S(2)}) copy-start(f32[64,16384]{1,0:T(8,128)} %get-tuple-element.166) | copy-start | bytes 12582916
